TPU v7x, 32 devices: a whole 2x2x4 slice. The times are simulated.
32 devices in a mesh: ctx: 2 (over x), fsdp: 16 (over z, y, core).
Axes of the slice: x: 2, y: 2, z: 4, core: 2. Of those that a mesh axis runs over, the one named last changes fastest.
Arguments:
- hidden_in: bfloat16 [16, 256, 1280], P('fsdp', 'ctx'), may hold values from -8 to 8
- values: bfloat16 [16, 256, 2560], P('fsdp', 'ctx'), may hold values from -6 to 6
- log_decay: float32 [16, 40, 256], P('fsdp', None, 'ctx'), may hold values from -1 to 0, as said below
- doc_lengths: int32 [16, 4], P('fsdp'), may hold values from 1 to 128, 256 in all within a row
- proj_bc: bfloat16 [1280, 256], P('fsdp'), may hold values from -0.15625 to 0.15625
- grad_out: bfloat16 [16, 256, 2560], P('fsdp', 'ctx'), may hold values from -6 to 6
Outputs:
- grad_values: bfloat16 [16, 256, 2560], P('fsdp', 'ctx')
- grad_hidden: bfloat16 [16, 256, 1280], P('fsdp', 'ctx')
- grad_proj: float32 [1280, 256], P('fsdp')
Inputs may be any that keep to these rules, and one draw needn't show every extreme that they name: `doc_lengths`: each sequence's 4 document lengths sum to 256; the longest is exactly half of 256. `log_decay`: logarithms of decays, all negative.
All inputs are finite; a program needn't handle non-finite values.
Results may differ from a plain program's by a relative error of at most 0.012.
Values may be sent and summed in bfloat16 or wider, within the bound.
A program may use at most 64 MiB of HBM per device.

v0:
```python
import jax
import jax.numpy as jnp
from jax import lax
from jax.sharding import PartitionSpec as P


def entering(value, axis, combine, identity, reverse):
    length, mine = (lax.axis_size(axis), lax.axis_index(axis))
    everything = jax.tree.map(
        lambda part, kind: lax.all_gather(part.astype(kind), axis),
        value,
        (jnp.bfloat16, jnp.bfloat16),
    )
    start = jax.tree.map(
        lambda part, zero: jnp.broadcast_to(jnp.asarray(zero, part.dtype), part.shape),
        value,
        identity,
    )

    def turn(k, before):
        at = length - 1 - k if reverse else k
        reached = at > mine if reverse else at < mine
        new = combine(
            before, jax.tree.map(lambda part, own: part[at].astype(own.dtype), everything, value)
        )
        return jax.tree.map(lambda a, b: jnp.where(reached, a, b), new, before)

    return lax.fori_loop(0, length, turn, start)


def combine_pairs(first_pair, second_pair):
    first_decay, first_state = first_pair
    second_decay, second_state = second_pair
    rows_count = first_state.shape[0]
    head_count = first_decay.shape[0]
    decayed = (
        first_state.reshape(rows_count, head_count, -1) * second_decay[None, :, None]
    ).reshape(first_state.shape)
    return (first_decay * second_decay, decayed + second_state)


def block_terms(b_rows, c_rows, value_rows, grad_rows, decay_rows, doc_ids, prev_doc):
    token_count, state_size = b_rows.shape
    head_count = decay_rows.shape[0]
    inner_width = value_rows.shape[1]
    head_dim = inner_width // head_count
    cumulative = jnp.cumsum(decay_rows, axis=1)
    last_doc = doc_ids[-1]
    token_places = jnp.arange(token_count, dtype=jnp.int32)
    allowed = (doc_ids[:, None] == doc_ids[None, :]) & (
        token_places[:, None] >= token_places[None, :]
    )
    spread = cumulative[:, :, None] - cumulative[:, None, :]
    decay_matrix = jnp.where(allowed[None], jnp.exp(jnp.where(allowed[None], spread, 0.0)), 0.0)
    in_weight = jnp.exp(cumulative) * (doc_ids == prev_doc).astype(jnp.float32)[None, :]
    out_weight = (
        jnp.exp(cumulative[:, -1:] - cumulative)
        * (doc_ids == last_doc).astype(jnp.float32)[None, :]
    )
    total_decay = jnp.exp(cumulative[:, -1]) * (last_doc == prev_doc).astype(jnp.float32)
    contract_last = (((1,), (1,)), ((), ()))
    scores = (
        lax.dot_general(c_rows, b_rows, contract_last, preferred_element_type=jnp.float32)
        / state_size
    )
    mixing = (decay_matrix * scores[None]).astype(jnp.bfloat16)
    value_heads = value_rows.reshape(token_count, head_count, head_dim)
    grad_heads = grad_rows.reshape(token_count, head_count, head_dim)
    products = jnp.einsum(
        "rhp,thp->hrt", grad_heads, value_heads, preferred_element_type=jnp.float32
    )
    kernel = (jnp.sum(decay_matrix * products, axis=0) / state_size).astype(jnp.bfloat16)
    grad_value_local = jnp.einsum(
        "hrt,rhp->thp", mixing, grad_heads, preferred_element_type=jnp.float32
    ).reshape(token_count, inner_width)
    contract_first = (((0,), (0,)), ((), ()))
    grad_b_local = lax.dot_general(
        kernel, c_rows, contract_first, preferred_element_type=jnp.float32
    )
    grad_c_local = jnp.dot(kernel, b_rows, preferred_element_type=jnp.float32)
    weighted_values = (
        (out_weight.T[:, :, None] * value_heads)
        .reshape(token_count, inner_width)
        .astype(jnp.bfloat16)
    )
    weighted_grads = (
        (in_weight.T[:, :, None] * grad_heads)
        .reshape(token_count, inner_width)
        .astype(jnp.bfloat16)
    )
    local_state = lax.dot_general(
        b_rows, weighted_values, contract_first, preferred_element_type=jnp.float32
    )
    local_grad = (
        lax.dot_general(c_rows, weighted_grads, contract_first, preferred_element_type=jnp.float32)
        / state_size
    )
    return (
        total_decay,
        local_state,
        local_grad,
        out_weight,
        weighted_values,
        weighted_grads,
        grad_value_local,
        grad_b_local,
        grad_c_local,
    )


def block_finish(b_rows, terms, state_in, grad_after):
    out_weight = terms[3]
    weighted_values = terms[4]
    weighted_grads = terms[5]
    grad_value_local = terms[6]
    grad_b_local = terms[7]
    grad_c_local = terms[8]
    token_count, state_size = b_rows.shape
    head_count = out_weight.shape[0]
    inner_width = weighted_values.shape[1]
    state_used = state_in.astype(jnp.bfloat16)
    grad_used = grad_after.astype(jnp.bfloat16)
    contract_last = (((1,), (1,)), ((), ()))
    grad_c_edge = (
        lax.dot_general(
            weighted_grads, state_used, contract_last, preferred_element_type=jnp.float32
        )
        / state_size
    )
    grad_b_edge = lax.dot_general(
        weighted_values, grad_used, contract_last, preferred_element_type=jnp.float32
    )
    edge_values = jnp.dot(b_rows, grad_used, preferred_element_type=jnp.float32).reshape(
        token_count, head_count, -1
    )
    grad_value_edge = (out_weight.T[:, :, None] * edge_values).reshape(token_count, inner_width)
    grad_values = (grad_value_local + grad_value_edge).astype(jnp.bfloat16)
    grad_bc = jnp.concatenate(
        [grad_b_local + grad_b_edge, grad_c_local + grad_c_edge], axis=1
    ).astype(jnp.bfloat16)
    return (grad_values, grad_bc)


def local(hidden_in, values, log_decay, doc_lengths, proj_bc, grad_out):
    token_count = hidden_in.shape[1]
    state_size = proj_bc.shape[1] // 2
    hidden_rows = hidden_in[0]
    first_proj = lax.all_gather(proj_bc, "fsdp", axis=0, tiled=True)
    projected = jnp.dot(hidden_rows, first_proj, preferred_element_type=jnp.float32).astype(
        jnp.bfloat16
    )
    b_rows = projected[:, :state_size]
    c_rows = projected[:, state_size:]
    lengths = doc_lengths[0]
    doc_starts = jnp.cumsum(lengths) - lengths
    first_token = lax.axis_index("ctx") * token_count
    token_places = first_token + jnp.arange(token_count, dtype=jnp.int32)
    doc_ids = jnp.sum((doc_starts[None, :] <= token_places[:, None]).astype(jnp.int32), axis=1)
    prev_doc = jnp.sum((doc_starts <= first_token - 1).astype(jnp.int32))
    terms = block_terms(b_rows, c_rows, values[0], grad_out[0], log_decay[0], doc_ids, prev_doc)
    total_decay = terms[0]
    unit_pair = (jnp.ones_like(total_decay), jnp.zeros_like(terms[1]))
    state_in = entering((total_decay, terms[1]), "ctx", combine_pairs, unit_pair, False)[1]
    grad_after = entering((total_decay, terms[2]), "ctx", combine_pairs, unit_pair, True)[1]
    grad_values, grad_bc = block_finish(b_rows, terms, state_in, grad_after)
    contract_last = (((1,), (1,)), ((), ()))
    grad_hidden = lax.dot_general(
        grad_bc, first_proj, contract_last, preferred_element_type=jnp.float32
    ).astype(jnp.bfloat16)
    seq_total = lax.axis_size("fsdp") * hidden_in.shape[0]
    contract_first = (((0,), (0,)), ((), ()))
    full_term = (
        lax.dot_general(hidden_rows, grad_bc, contract_first, preferred_element_type=jnp.float32)
        / seq_total
    )
    summed = lax.psum(full_term, "ctx")
    grad_proj = lax.psum_scatter(summed, "fsdp", scatter_dimension=0, tiled=True)
    return (grad_values[None], grad_hidden[None], grad_proj)


def solution(mesh):
    in_specs = (
        P("fsdp", "ctx", None),
        P("fsdp", "ctx", None),
        P("fsdp", None, "ctx"),
        P("fsdp", None),
        P("fsdp", None),
        P("fsdp", "ctx", None),
    )
    out_specs = (P("fsdp", "ctx", None), P("fsdp", "ctx", None), P("fsdp", None))
    return jax.shard_map(local, mesh=mesh, in_specs=in_specs, out_specs=out_specs, check_vma=False)
```

profile of v0, /device:TPU:0, one launch (start us, length us, event | category | flops | bytes accessed | tf_op | source)
XLA Modules:
  0.0 186.9 jit_solution(2364739231670539729)
XLA Ops:
  9.4 1.3 fusion.33
  11.9 1.4 copy.36
  13.4 25.1 %all_gather.21 = bf16[1280,256]{1,0:T(8,128)(2,1)S(1)} all-gather(bf16[80,256]{1,0:T(8,128)(2,1)S(1)} %copy-done.8), channel_id=1, replica_groups=mesh['ctx'=2,'fsdp'=16] {'fsdp'}, dimensions={0}, use_global_device_ids=true | all-gather | bytes 696320 | tf_op jit(solution)/shard_map/all_gather | solution.py:148
  48.0 5.1 %all-reduce = bf16[80]{0:T(256)(128)(2,1)S(1)} all-reduce(bf16[80]{0:T(256)(128)(2,1)S(1)} %dynamic-update-slice), channel_id=2, replica_groups=mesh['ctx'=2,'fsdp'=16] {'ctx'}, use_global_device_ids=true, to_apply=%add | all-reduce | flops 80 | bytes 320
  53.2 2.4 %multiply_reduce_fusion = f32[128,128]{1,0:T(8,128)S(1)} fusion(bf16[128,40,64]{0,2,1:T(8,128)(2,1)} %bitcast.81, bf16[128,40,64]{0,2,1:T(8,128)(2,1)} %bitcast.83, f32[40,128]{1,0:T(8,128)S(1)} %reduce_window_sum.18, pred[128,128]{1,0:T(8,128)(4,1)S(1)} %fusion.24), kind=kOutput, calls=%fused_computation.15 | convolution fusion | flops 87146496 | bytes 1413120 | tf_op jit(solution)/shard_map/rhp,thp->hrt/dot_general | solution.py:69
  55.7 8.2 %all-gather.6.cloned.1.call-done = bf16[256,2560]{1,0:T(8,128)(2,1)} async-done(((bf16[128,2560]{1,0:T(8,128)(2,1)}), bf16[256,2560]{1,0:T(8,128)(2,1)}) %all-gather.6.cloned.1.call-update) | async-done | bytes 1310736 | tf_op jit(solution)/shard_map/all_gather | solution.py:10
  63.8 4.2 %while.30 = (s32[]{:T(128)}, f32[128,2560]{1,0:T(8,128)S(1)}, s32[]{:T(128)}, bf16[2,40]{1,0:T(2,128)(2,1)S(1)}, bf16[2,128,2560]{2,1,0:T(8,128)(2,1)}, /*index=5*/s32[]{:T(128)}, s32[]{:T(128)}, s32[]{:T(128)}) while((s32[]{:T(128)}, f32[128,2560]{1,0:T(8,128)S(1)}, s32[]{:T(128)}, bf16[2,40]{1,0:T(2,128)(2,1)S(1)}, ...), condition=%wide.region_5.6_spmd.clone, body=%wide.region_4.5_spmd.clone.sunk | while | flops 1638448 | bytes 3318319 | solution.py:28
  64.0 1.9 %fusion.51 = f32[128,2560]{1,0:T(8,128)S(1)} fusion(f32[128,2560]{1,0:T(8,128)S(1)} %get-tuple-element.374, bf16[2,128,2560]{2,1,0:T(8,128)(2,1)} %get-tuple-element.385, s32[]{:T(128)S(6)} %select_n.90, f32[2560]{0:T(1024)S(1)} %mul.207, pred[]{:T(512)S(6)} %compare.6, pred[]{:T(512)S(6)} %gt.12), kind=kLoop, calls=%fused_computation.1.clone.1 | loop fusion | flops 1638400 | bytes 3287046 | tf_op jit(solution)/shard_map/while/body/eval_jaxpr/jit(_where)/select_n | solution.py:26
  66.1 1.9 %fusion.51 = f32[128,2560]{1,0:T(8,128)S(1)} fusion(f32[128,2560]{1,0:T(8,128)S(1)} %get-tuple-element.374, bf16[2,128,2560]{2,1,0:T(8,128)(2,1)} %get-tuple-element.385, s32[]{:T(128)S(6)} %select_n.90, f32[2560]{0:T(1024)S(1)} %mul.207, pred[]{:T(512)S(6)} %compare.6, pred[]{:T(512)S(6)} %gt.12), kind=kLoop, calls=%fused_computation.1.clone.1 | loop fusion | flops 1638400 | bytes 3287046 | tf_op jit(solution)/shard_map/while/body/eval_jaxpr/jit(_where)/select_n | solution.py:26
  68.0 1.5 fusion.21
  69.5 20.1 %all-gather.8.cloned.1.call-done = bf16[256,2560]{1,0:T(8,128)(2,1)} async-done(((bf16[128,2560]{1,0:T(8,128)(2,1)}), bf16[256,2560]{1,0:T(8,128)(2,1)}) %all-gather.8.cloned.1.call-update) | async-done | bytes 1310736 | tf_op jit(solution)/shard_map/all_gather | solution.py:10
  89.6 4.2 %while.31 = (s32[]{:T(128)}, f32[128,2560]{1,0:T(8,128)S(1)}, s32[]{:T(128)}, bf16[2,40]{1,0:T(2,128)(2,1)S(1)}, bf16[2,128,2560]{2,1,0:T(8,128)(2,1)}, /*index=5*/s32[]{:T(128)}, s32[]{:T(128)}) while((s32[]{:T(128)}, f32[128,2560]{1,0:T(8,128)S(1)}, s32[]{:T(128)}, bf16[2,40]{1,0:T(2,128)(2,1)S(1)}, ...), condition=%wide.region_8.9_spmd.clone, body=%wide.region_7.8_spmd.clone.sunk | while | flops 1638444 | bytes 3318265 | solution.py:28
  89.7 1.9 %fusion.52 = f32[128,2560]{1,0:T(8,128)S(1)} fusion(f32[128,2560]{1,0:T(8,128)S(1)} %get-tuple-element.397, bf16[2,128,2560]{2,1,0:T(8,128)(2,1)} %get-tuple-element.407, s32[]{:T(128)} %get-tuple-element.396, f32[2560]{0:T(1024)S(1)} %mul.211, pred[]{:T(512)S(6)} %compare.7, pred[]{:T(512)S(6)} %lt.45), kind=kLoop, calls=%fused_computation.4.clone.1 | loop fusion | flops 1638400 | bytes 3287046 | tf_op jit(solution)/shard_map/while/body/eval_jaxpr/jit(_where)/select_n | solution.py:26
  91.8 1.9 %fusion.52 = f32[128,2560]{1,0:T(8,128)S(1)} fusion(f32[128,2560]{1,0:T(8,128)S(1)} %get-tuple-element.397, bf16[2,128,2560]{2,1,0:T(8,128)(2,1)} %get-tuple-element.407, s32[]{:T(128)} %get-tuple-element.396, f32[2560]{0:T(1024)S(1)} %mul.211, pred[]{:T(512)S(6)} %compare.7, pred[]{:T(512)S(6)} %lt.45), kind=kLoop, calls=%fused_computation.4.clone.1 | loop fusion | flops 1638400 | bytes 3287046 | tf_op jit(solution)/shard_map/while/body/eval_jaxpr/jit(_where)/select_n | solution.py:26
  93.7 1.5 convolution_multiply_fusion.4
  95.9 1.5 copy.51
  97.5 1.5 copy.38
  99.1 2.3 %fusion.8 = f32[40,128,64]{1,2,0:T(8,128)S(1)} fusion(bf16[128,40,64]{0,2,1:T(8,128)(2,1)} %bitcast.82, f32[128,128]{1,0:T(8,128)S(1)} %convolution_multiply_fusion.3, f32[40,128]{1,0:T(8,128)S(1)} %reduce_window_sum.18, pred[128,128]{1,0:T(8,128)(4,1)S(1)} %fusion.24), kind=kOutput, calls=%fused_computation.20 | convolution fusion | flops 87162880 | bytes 2068480 | tf_op jit(solution)/shard_map/hrt,rhp->thp/dot_general | solution.py:73
  101.4 1.5 copy.39
  102.9 3.0 %fusion.5 = bf16[1,128,2560]{2,1,0:T(8,128)(2,1)} fusion(f32[128,2560]{1,0:T(8,128)} %copy.39, f32[128,2560]{1,0:T(8,128)} %copy.38, f32[128,2560]{1,0:T(8,128)S(1)} %get-tuple-element.229, bf16[128,256]{1,0:T(8,128)(2,1)S(1)} %convolution_convert_fusion.2), kind=kOutput, calls=%fused_computation.12 | convolution fusion | flops 85196800 | bytes 4620288 | tf_op jit(solution)/shard_map/dot_general | solution.py:133
  105.9 50.3 %reduce-scatter.4.cloned.1.call-done = f32[80,256]{1,0:T(8,128)} async-done(((f32[1280,256]{1,0:T(8,128)}), f32[80,256]{1,0:T(8,128)}) %reduce-scatter.4.cloned.1.call-update) | async-done | bytes 81936
  156.1 1.6 copy.52
  158.9 19.9 %all-reduce.3.cloned.1.call-done = f32[80,256]{0,1:T(8,128)} async-done(((f32[80,256]{0,1:T(8,128)}), f32[80,256]{0,1:T(8,128)}) %all-reduce.3.cloned.1.call-update) | async-done | bytes 81936 | tf_op jit(solution)/shard_map/psum | solution.py:176
  178.8 1.6 copy.46
  (69 shorter events, 13.6 us)
Async XLA Ops:
  7.2 32.9 %copy-start = (bf16[1,128,1280]{2,1,0:T(8,128)(2,1)S(1)}, bf16[1,128,1280]{2,1,0:T(8,128)(2,1)}, u32[]{:S(2)}) copy-start(bf16[1,128,1280]{2,1,0:T(8,128)(2,1)} %param.10) | copy-start | bytes 983044
  7.2 6.2 %copy-start.8 = (bf16[80,256]{1,0:T(8,128)(2,1)S(1)}, bf16[80,256]{1,0:T(8,128)(2,1)}, u32[]{:S(2)}) copy-start(bf16[80,256]{1,0:T(8,128)(2,1)} %param.14) | copy-start | bytes 122884
  7.2 56.7 %all-gather.6.cloned.1.call-start = ((), (), s32[]{:S(2)}) async-start(), calls=%async_computation.1 | async-start | bytes 1966080 | tf_op jit(solution)/shard_map/all_gather | solution.py:10
  13.3 27.0 %copy-start.5 = (bf16[1,128,2560]{1,2,0:T(8,128)(2,1)}, bf16[1,128,2560]{1,2,0:T(8,128)(2,1)S(1)}, u32[]{:S(2)}) copy-start(bf16[1,128,2560]{1,2,0:T(8,128)(2,1)S(1)} %copy.36) | copy-start | bytes 1966084
  38.5 1.5 copy-start.3
  40.0 0.8 copy-start.1
  40.0 2.1 %copy-start.7 = (bf16[1,128,2560]{2,1,0:T(8,128)(2,1)S(1)}, bf16[1,128,2560]{2,1,0:T(8,128)(2,1)}, u32[]{:S(2)}) copy-start(bf16[1,128,2560]{2,1,0:T(8,128)(2,1)} %param.11) | copy-start | bytes 1966084
  42.1 47.4 %all-gather.8.cloned.1.call-start = ((), (), s32[]{:S(2)}) async-start(), calls=%async_computation.2 | async-start | bytes 1966080 | tf_op jit(solution)/shard_map/all_gather | solution.py:10
  42.5 2.3 %copy-start.6 = (bf16[1,128,2560]{1,2,0:T(8,128)(2,1)}, bf16[1,128,2560]{1,2,0:T(8,128)(2,1)S(1)}, u32[]{:S(2)}) copy-start(bf16[1,128,2560]{1,2,0:T(8,128)(2,1)S(1)} %copy.40) | copy-start | bytes 1966084
  42.6 0.9 copy-start.2
  43.6 2.9 %copy-start.9 = (u32[32]{0:T(128)S(1)}, u32[32]{0:T(128)}, u32[]{:S(2)}) copy-start(u32[32]{0:T(128)} %constant.94) | copy-start | bytes 388
  44.8 111.3 %reduce-scatter.4.cloned.1.call-start = ((), (), s32[]{:S(2)}) async-start(), calls=%async_computation.4 | async-start | bytes 1392640
  97.4 81.4 %all-reduce.3.cloned.1.call-start = ((), (), s32[]{:S(2)}) async-start(), calls=%async_computation.3 | async-start | bytes 262144 | tf_op jit(solution)/shard_map/psum | solution.py:176
  102.9 54.9 %copy-start.4 = (bf16[1280,256]{1,0:T(8,128)(2,1)S(1)}, bf16[1280,256]{1,0:T(8,128)(2,1)}, u32[]{:S(2)}) copy-start(bf16[1280,256]{1,0:T(8,128)(2,1)} %copy-done.3) | copy-start | bytes 1966084
Sparse Core Ops, SparseCore 0:
  42.2 21.5 all-gather.5
  65.4 24.1 all-gather.7
  97.5 58.5 reduce-scatter.3
  158.2 20.5 all-reduce.2
where the time goes:
time: 188 us; the launch traced here: 187 us
  waiting for transfers between devices  98.5 us (52%)
  blocking collectives  30.2 us (16%)
  between operations  16 us (9%)
  matrix products  15.2 us (8%)
  local copies, waits for them, and re-layouts  13.4 us (7%)
  other arithmetic  13.4 us (7%)
    unnamed x5, waiting for transfers between devices  50.3 us
    all_gather x2, waiting for transfers between devices, entering(): lax.all_gather(part.astype(kind), axis)  28.3 us
    all_gather x1, blocking collectives, local(): first_proj = lax.all_gather(proj_bc, 'fsdp', axis=0, tiled=True)  25.1 us
    psum x1, waiting for transfers between devices, local(): summed = lax.psum(full_term, 'ctx')  19.9 us
    unnamed x28, local copies, waits for them, and re-layouts  8.88 us
    select_n x4, other arithmetic, turn(): return jax.tree.map(lambda a, b: jnp.where(reached, a, b), new, before)  7.64 us
    unnamed x1, blocking collectives  5.12 us
  transfers between devices with their start and end apart: 4, of which 4 were waited for; matrix products, arithmetic and copies ran while one was open for 11% of the time, Pallas kernels for 0%

commit v1 on v0

--- a/solution.py
+++ b/solution.py
@@ -1,7 +1,284 @@
+import functools
+
 import jax
 import jax.numpy as jnp
 from jax import lax
+from jax.experimental import pallas as pl
+from jax.experimental.pallas import tpu as pltpu
 from jax.sharding import PartitionSpec as P
+
+F32 = jnp.float32
+BF16 = jnp.bfloat16
+NN = (((1,), (0,)), ((), ()))
+NT = (((1,), (1,)), ((), ()))
+VM = pl.BlockSpec(memory_space=pltpu.VMEM)
+SM = pl.BlockSpec(memory_space=pltpu.SMEM)
+
+
+def mm(a, b, dims=NN):
+    return lax.dot_general(a, b, dims, preferred_element_type=F32)
+
+
+def send(src, dst, s, r, device):
+    return pltpu.make_async_remote_copy(
+        src_ref=src,
+        dst_ref=dst,
+        send_sem=s,
+        recv_sem=r,
+        device_id=device,
+        device_id_type=pl.DeviceIdType.MESH,
+    )
+
+
+def greet(devices):
+    barrier = pltpu.get_barrier_semaphore()
+    for device in devices:
+        pl.semaphore_signal(
+            barrier, inc=1, device_id=device, device_id_type=pl.DeviceIdType.MESH
+        )
+    pl.semaphore_wait(barrier, len(devices))
+
+
+def gather_kernel(n, x_ref, o_ref, s1, r1, s2, r2, own_sem):
+    me = lax.axis_index("fsdp")
+    half = n // 2
+    mate = {"fsdp": me + 1 - 2 * (me % 2)}
+    peers = [{"fsdp": (me + 2 * k) % n} for k in range(1, half)]
+    greet([mate] + peers)
+    own = pltpu.make_async_copy(x_ref, o_ref.at[me], own_sem)
+    own.start()
+    first = [send(x_ref, o_ref.at[me], s1.at[k], r1.at[k], p) for k, p in enumerate(peers)]
+    for copy in first:
+        copy.start()
+    second = [send(x_ref, o_ref.at[me], s2.at[0], r2.at[0], mate)]
+    second[0].start()
+    for k in range(1, half):
+        block = o_ref.at[(me + n - 2 * k) % n]
+        send(x_ref, block, s1.at[k - 1], r1.at[k - 1], peers[k - 1]).wait_recv()
+        second.append(send(block, block, s2.at[k], r2.at[k], mate))
+        second[k].start()
+    own.wait()
+    for copy in first:
+        copy.wait_send()
+    for k in range(half):
+        second[k].wait_send()
+        block = o_ref.at[(mate["fsdp"] + n - 2 * k) % n]
+        send(x_ref, block, s2.at[k], r2.at[k], mate).wait_recv()
+
+
+def gather(shard, n):
+    sems = [pltpu.SemaphoreType.DMA((n // 2,))] * 4 + [pltpu.SemaphoreType.DMA]
+    whole = pl.pallas_call(
+        functools.partial(gather_kernel, n),
+        out_shape=jax.ShapeDtypeStruct((n,) + shard.shape, shard.dtype),
+        in_specs=[VM],
+        out_specs=VM,
+        scratch_shapes=sems,
+        compiler_params=pltpu.CompilerParams(collective_id=0, has_side_effects=True),
+        name="gather_proj",
+    )(shard)
+    return whole.reshape(-1, shard.shape[1])
+
+
+def scatter_kernel(n, x_ref, o_ref, a_ref, y_ref, z_ref, w_ref, u_ref, s1, r1, s2, r2, s3, r3):
+    me = lax.axis_index("fsdp")
+    half = n // 2
+    par = me % 2
+    mine = me // 2
+    mate = {"fsdp": me + 1 - 2 * par}
+    across = {"ctx": 1 - lax.axis_index("ctx")}
+    spots = [(mine + k + 1) % half for k in range(half)]
+    peers = [{"fsdp": 2 * j + par} for j in spots[:-1]]
+    greet([mate, across] + peers)
+    first = [
+        send(x_ref.at[j, 1 - par], a_ref.at[k], s1.at[k], r1.at[k], mate)
+        for k, j in enumerate(spots)
+    ]
+    for copy in first:
+        copy.start()
+    second = []
+    for k in range(half - 1):
+        first[k].wait_recv()
+        y_ref[k] = (x_ref[spots[k], par].astype(F32) + a_ref[k].astype(F32)).astype(BF16)
+        second.append(send(y_ref.at[k], z_ref.at[k], s2.at[k], r2.at[k], peers[k]))
+        second[k].start()
+    first[half - 1].wait_recv()
+    total = x_ref[mine, par].astype(F32) + a_ref[half - 1].astype(F32)
+    for copy in first:
+        copy.wait_send()
+    for k in range(half - 1):
+        second[k].wait()
+        total = total + z_ref[k].astype(F32)
+    w_ref[...] = total
+    last = send(w_ref, u_ref, s3, r3, across)
+    last.start()
+    last.wait()
+    o_ref[...] = w_ref[...] + u_ref[...]
+
+
+def scatter_sum(term, n):
+    rows, cols = term.shape[0] // n, term.shape[1]
+    half = n // 2
+    return pl.pallas_call(
+        functools.partial(scatter_kernel, n),
+        out_shape=jax.ShapeDtypeStruct((rows, cols), F32),
+        in_specs=[VM],
+        out_specs=VM,
+        scratch_shapes=[pltpu.VMEM((half, rows, cols), BF16)] * 3
+        + [pltpu.VMEM((rows, cols), F32)] * 2
+        + [pltpu.SemaphoreType.DMA((half,))] * 4
+        + [pltpu.SemaphoreType.DMA] * 2,
+        compiler_params=pltpu.CompilerParams(collective_id=1, has_side_effects=True),
+        name="scatter_proj",
+    )(term.reshape(half, 2, rows, cols))
+
+
+def doc_of(lengths_ref, places):
+    start, count = jnp.int32(0), jnp.zeros(places.shape, jnp.int32)
+    for k in range(lengths_ref.shape[1]):
+        count = count + (start <= places).astype(jnp.int32)
+        start = start + lengths_ref[0, k]
+    return count
+
+
+def prefix_sums(decay_ref):
+    tokens = decay_ref.shape[1]
+    r = lax.broadcasted_iota(jnp.int32, (tokens, tokens), 0)
+    t = lax.broadcasted_iota(jnp.int32, (tokens, tokens), 1)
+    exact = functools.partial(
+        lax.dot_general, precision=lax.Precision.HIGHEST, preferred_element_type=F32
+    )
+    rows = exact(decay_ref[...], (r <= t).astype(F32), NN)
+    columns = exact((r >= t).astype(F32), decay_ref[...], NT)
+    return rows, columns
+
+
+def spread_pair(weights, h, low):
+    return jnp.where(low, weights[:, h : h + 1], weights[:, h + 1 : h + 2])
+
+
+def out_weights(columns, lengths_ref, first_token):
+    tokens = columns.shape[0]
+    places = lax.broadcasted_iota(jnp.int32, columns.shape, 0) + first_token
+    docs = doc_of(lengths_ref, places)
+    last = doc_of(lengths_ref, jnp.full(columns.shape, first_token + tokens - 1, jnp.int32))
+    return docs, jnp.where(docs == last, jnp.exp(columns[tokens - 1 :, :] - columns), 0.0)
+
+
+def start_kernel(len_ref, hid_ref, proj_ref, val_ref, grad_ref, dec_ref, bc_ref, pay_ref, sel_ref):
+    tokens, state = hid_ref.shape[0], proj_ref.shape[1] // 2
+    lead = lax.axis_index("ctx") == 0
+    first_token = lax.axis_index("ctx") * tokens
+    bc = mm(hid_ref[...], proj_ref[...]).astype(BF16)
+    bc_ref[...] = bc
+    _, columns = prefix_sums(dec_ref)
+    docs, out_w = out_weights(columns, len_ref, first_token)
+    prev = doc_of(len_ref, jnp.full(columns.shape, first_token - 1, jnp.int32))
+    in_w = jnp.where(docs == prev, jnp.exp(columns), 0.0)
+    lead_v = jnp.full((tokens, state), lead.astype(jnp.int32), jnp.int32) == 1
+    weights = jnp.where(lead_v[:, : columns.shape[1]], out_w, in_w)
+    side = jnp.where(lead_v, bc[:, :state].astype(F32), bc[:, state:].astype(F32))
+    turned = (side.T).astype(BF16)
+    scale = jnp.where(lead, 1.0, 1.0 / state).astype(F32)
+    low = lax.broadcasted_iota(jnp.int32, (tokens, 128), 1) < 64
+    for p in range(val_ref.shape[1] // 128):
+        at = slice(128 * p, 128 * p + 128)
+        raw = jnp.where(lead_v, val_ref[:, at].astype(F32), grad_ref[:, at].astype(F32))
+        weighted = (raw * spread_pair(weights, 2 * p, low)).astype(BF16)
+        sel_ref[:, at] = weighted
+        pay_ref[:, at] = (mm(turned, weighted) * scale).astype(BF16)
+
+
+def middle_kernel(len_ref, bc_ref, val_ref, grad_ref, dec_ref, gv_ref, gbc_ref):
+    tokens, state = bc_ref.shape[0], bc_ref.shape[1] // 2
+    first_token = lax.axis_index("ctx") * tokens
+    rows, columns = prefix_sums(dec_ref)
+    t = lax.broadcasted_iota(jnp.int32, (tokens, tokens), 0)
+    r = lax.broadcasted_iota(jnp.int32, (tokens, tokens), 1)
+    allowed = (doc_of(len_ref, t + first_token) == doc_of(len_ref, r + first_token)) & (r >= t)
+    b, c = bc_ref[:, :state], bc_ref[:, state:]
+    scores = mm(b, c, NT) / state
+    low = lax.broadcasted_iota(jnp.int32, (tokens, 128), 1) < 64
+    none = jnp.zeros((tokens, 128), BF16)
+    kernel = jnp.zeros((tokens, tokens), F32)
+    for p in range(val_ref.shape[1] // 128):
+        at = slice(128 * p, 128 * p + 128)
+        v, g = val_ref[:, at], grad_ref[:, at]
+        split_v = jnp.concatenate([jnp.where(low, v, none), jnp.where(low, none, v)], axis=0)
+        split_g = jnp.concatenate([jnp.where(low, g, none), jnp.where(low, none, g)], axis=0)
+        products = mm(split_v, g, NT)
+        mixes = []
+        for i in range(2):
+            h = 2 * p + i
+            spread = rows[h : h + 1, :] - columns[:, h : h + 1]
+            decay = jnp.exp(jnp.where(allowed, spread, -1e30))
+            kernel = kernel + decay * products[i * tokens : (i + 1) * tokens, :]
+            mixes.append((decay * scores).astype(BF16))
+        gv_ref[:, at] = mm(jnp.concatenate(mixes, axis=1), split_g)
+    kernel = kernel / state
+    gbc_ref[:, :state] = mm(kernel.astype(BF16), c)
+    gbc_ref[:, state:] = mm(kernel.T.astype(BF16), b)
+
+
+def end_kernel(
+    seq_total, len_ref, got_ref, sel_ref, gv_ref, gbc_ref, bc_ref, dec_ref, proj_ref, hid_ref,
+    out_ref, hidden_ref, term_ref,
+):
+    tokens, state = bc_ref.shape[0], bc_ref.shape[1] // 2
+    lead = (lax.axis_index("ctx") == 0).astype(F32)
+    _, columns = prefix_sums(dec_ref)
+    _, out_w = out_weights(columns, len_ref, lax.axis_index("ctx") * tokens)
+    out_w = out_w * lead
+    low = lax.broadcasted_iota(jnp.int32, (tokens, 128), 1) < 64
+    edge = mm(sel_ref[...], got_ref[...], NT)
+    b = bc_ref[:, :state]
+    for p in range(got_ref.shape[1] // 128):
+        at = slice(128 * p, 128 * p + 128)
+        more = mm(b, got_ref[:, at]) * spread_pair(out_w, 2 * p, low)
+        out_ref[:, at] = (gv_ref[:, at] + more).astype(BF16)
+    gb = (gbc_ref[:, :state] + edge * lead).astype(BF16)
+    gc = (gbc_ref[:, state:] + edge * ((1.0 - lead) / state)).astype(BF16)
+    gbc = jnp.concatenate([gb, gc], axis=1)
+    hidden_ref[...] = mm(gbc, proj_ref[...], NT).astype(BF16)
+    turned = hid_ref[...].astype(F32).T.astype(BF16)
+    term_ref[...] = (mm(turned, gbc) / seq_total).astype(BF16)
+
+
+def call(body, name, flops, outs, *args):
+    shapes = tuple(jax.ShapeDtypeStruct(s, d) for s, d in outs)
+    return pl.pallas_call(
+        body,
+        out_shape=shapes,
+        in_specs=[SM] + [VM] * (len(args) - 1),
+        out_specs=tuple(VM for _ in shapes),
+        cost_estimate=pl.CostEstimate(flops=flops, bytes_accessed=4000000, transcendentals=0),
+        name=name,
+    )(*args)
+
+
+def paired(hidden_in, values, log_decay, doc_lengths, proj_bc, grad_out):
+    n = lax.axis_size("fsdp")
+    hid, val, dec, grad = hidden_in[0], values[0], log_decay[0], grad_out[0]
+    tokens, inner = val.shape
+    wide = proj_bc.shape[1]
+    proj = gather(proj_bc, n)
+    bc, pay, sel = call(
+        start_kernel, "start", 200000000,
+        [((tokens, wide), BF16), ((wide // 2, inner), BF16), ((tokens, inner), BF16)],
+        doc_lengths, hid, proj, val, grad, dec,
+    )
+    got = lax.ppermute(pay, "ctx", [(0, 1), (1, 0)])
+    gv, gbc = call(
+        middle_kernel, "middle", 4000000000,
+        [((tokens, inner), F32), ((tokens, wide), F32)],
+        doc_lengths, bc, val, grad, dec,
+    )
+    out, hidden, term = call(
+        functools.partial(end_kernel, n * hidden_in.shape[0]), "end", 400000000,
+        [((tokens, inner), BF16), (hid.shape, BF16), ((hid.shape[1], wide), BF16)],
+        doc_lengths, got, sel, gv, gbc, bc, dec, proj, hid,
+    )
+    return (out[None], hidden[None], scatter_sum(term, n))
 
 
 def entering(value, axis, combine, identity, reverse):
@@ -188,4 +465,5 @@
         P("fsdp", "ctx", None),
     )
     out_specs = (P("fsdp", "ctx", None), P("fsdp", "ctx", None), P("fsdp", None))
-    return jax.shard_map(local, mesh=mesh, in_specs=in_specs, out_specs=out_specs, check_vma=False)
+    body = paired if mesh.shape["ctx"] == 2 and mesh.shape["fsdp"] % 2 == 0 else local
+    return jax.shard_map(body, mesh=mesh, in_specs=in_specs, out_specs=out_specs, check_vma=False)

time: 188 us -> 61.8 us (0.33)
  waiting for transfers between devices: 98.5 us -> 11.7 us
  Pallas kernels: 0 us -> 45.3 us
  blocking collectives: 30.2 us -> 0 us
  between operations: 16 us -> 0.65 us
  matrix products: 15.2 us -> 0 us
  other arithmetic: 13.4 us -> 0 us
  local copies, waits for them, and re-layouts: 13.4 us -> 2.36 us
    unnamed x5 -> x0, waiting for transfers between devices: 50.3 us -> none
    pallas_call x0 -> x5, Pallas kernels: none -> 45.3 us  [the longest x1 18.4 us: scatter_sum(): pl.pallas_call(functools.partial(scatter_kernel, n), out_shape=jax.ShapeD...]
    all_gather x2 -> x0, waiting for transfers between devices: 28.3 us -> none  [entering(): lax.all_gather(part.astype(kind), axis)]
    all_gather x1 -> x0, blocking collectives: 25.1 us -> none  [local(): first_proj = lax.all_gather(proj_bc, 'fsdp', axis=0, tiled=True)]
    psum x1 -> x0, waiting for transfers between devices: 19.9 us -> none  [local(): summed = lax.psum(full_term, 'ctx')]
    dot_general x13 -> x0, matrix products: 15.2 us -> none  [the longest x1 2.97 us: block_finish(): jnp.dot(b_rows, grad_used, preferred_element_type=jnp.float32)]
    ppermute x0 -> x1, waiting for transfers between devices: none -> 11.7 us  [paired(): got = lax.ppermute(pay, 'ctx', [(0, 1), (1, 0)])]
    select_n x4 -> x0, other arithmetic: 7.64 us -> none  [turn(): return jax.tree.map(lambda a, b: jnp.where(reached, a, b), new, before)]
  transfers between devices with their start and end apart: 4 -> 1, of which waited for: 4 -> 1; matrix products, arithmetic and copies ran while one was open for 11% -> 0% of each run, Pallas kernels for 0% -> 7%
where the time goes in v1:
time: 61.8 us; the launch traced here: 61.5 us
  Pallas kernels  45.3 us (73%)
  waiting for transfers between devices  11.7 us (19%)
  local copies, waits for them, and re-layouts  2.36 us (4%)
  starting transfers between devices  1.49 us (2%)
  between operations  0.65 us (1%)
    pallas_call x1, Pallas kernels, scatter_sum(): pl.pallas_call(functools.partial(scatter_kernel, n), out_shape=jax.ShapeD...  18.4 us
    pallas_call x1, Pallas kernels, gather(): pl.pallas_call(functools.partial(gather_kernel, n), out_shape=jax.ShapeDt...  14.9 us
    pallas_call x3, Pallas kernels, call(): pl.pallas_call(body, out_shape=shapes, in_specs=[SM] + [VM] * (len(args)...  12 us
    ppermute x1, waiting for transfers between devices, paired(): got = lax.ppermute(pay, 'ctx', [(0, 1), (1, 0)])  11.7 us
    unnamed x3, local copies, waits for them, and re-layouts  2.36 us
    ppermute x1, starting transfers between devices, paired(): got = lax.ppermute(pay, 'ctx', [(0, 1), (1, 0)])  1.49 us
  transfers between devices with their start and end apart: 1, of which 1 were waited for; matrix products, arithmetic and copies ran while one was open for 0% of the time, Pallas kernels for 7%

profile of v1, /device:TPU:0, one launch (start us, length us, event | category | flops | bytes accessed | tf_op | source)
XLA Modules:
  0.0 61.5 jit_solution(2979853084371378547)
XLA Ops:
  0.6 14.9 %gather_proj.1 = bf16[16,80,256]{2,1,0:T(8,128)(2,1)} custom-call(bf16[80,256]{1,0:T(8,128)(2,1)} %x_ref.1), custom_call_target="tpu_custom_call" | custom-call | tf_op jit(solution)/shard_map/gather_proj/pallas_call | solution.py:71
  15.5 3.9 %start.1 = (bf16[128,256]{1,0:T(8,128)(2,1)}, bf16[128,2560]{1,0:T(8,128)(2,1)}, bf16[128,2560]{1,0:T(8,128)(2,1)}) custom-call(s32[1,4]{1,0:T(1,128)} %len_ref.5, bf16[128,1280]{1,0:T(8,128)(2,1)} %bitcast.10, bf16[1280,256]{1,0:T(8,128)(2,1)} %bitcast.8, bf16[128,2560]{1,0:T(8,128)(2,1)} %bitcast.12, bf16[128,2560]{1,0:T(8,128)(2,1)} %bitcast.14, ...), custom_call_target="tpu_custom_call" | custom-call | flops 200000000 | bytes 4000000 | tf_op jit(solution)/shard_map/start/pallas_call | solution.py:249
  19.5 1.5 %collective-permute-start = (bf16[128,2560]{1,0:T(8,128)(2,1)}, bf16[128,2560]{1,0:T(8,128)(2,1)S(1)}, u32[]{:S(2)}, u32[]{:S(2)}) collective-permute-start(bf16[128,2560]{1,0:T(8,128)(2,1)} %get-tuple-element.11), channel_id=1, source_target_pairs={{0,16},{16,0},{1,17},{17,1},{2,18},{18,2},{3,19},{19,3},{4,20},{20... | collective-permute-start | bytes 1966088 | tf_op jit(solution)/shard_map/ppermute | solution.py:270
  21.0 4.0 %middle.1 = (f32[128,2560]{1,0:T(8,128)}, f32[128,256]{1,0:T(8,128)}) custom-call(s32[1,4]{1,0:T(1,128)} %len_ref.5, bf16[128,256]{1,0:T(8,128)(2,1)} %get-tuple-element.13.bc_ref, bf16[128,2560]{1,0:T(8,128)(2,1)} %bitcast.13, bf16[128,2560]{1,0:T(8,128)(2,1)} %bitcast.15, f32[40,128]{1,0:T(8,128)} %bitcast.18), custom_call_target="tpu_custom_call" | custom-call | flops 4000000000 | bytes 4000000 | tf_op jit(solution)/shard_map/middle/pallas_call | solution.py:249
  25.0 11.7 %collective-permute-done.got_ref = bf16[128,2560]{1,0:T(8,128)(2,1)S(1)} collective-permute-done((bf16[128,2560]{1,0:T(8,128)(2,1)}, bf16[128,2560]{1,0:T(8,128)(2,1)S(1)}, u32[]{:S(2)}, u32[]{:S(2)}) %collective-permute-start) | collective-permute-done | bytes 655392 | tf_op jit(solution)/shard_map/ppermute | solution.py:270
  36.7 0.0 copy-start
  36.7 0.8 %copy-done = bf16[128,2560]{1,0:T(8,128)(2,1)} copy-done((bf16[128,2560]{1,0:T(8,128)(2,1)}, bf16[128,2560]{1,0:T(8,128)(2,1)S(1)}, u32[]{:S(2)}) %copy-start) | copy-done | bytes 655384
  37.5 4.0 %end.1 = (bf16[128,2560]{1,0:T(8,128)(2,1)}, bf16[128,1280]{1,0:T(8,128)(2,1)}, bf16[1280,256]{1,0:T(8,128)(2,1)}) custom-call(s32[1,4]{1,0:T(1,128)} %len_ref.5, bf16[128,2560]{1,0:T(8,128)(2,1)} %copy-done, bf16[128,2560]{1,0:T(8,128)(2,1)} %get-tuple-element.12.sel_ref, f32[128,2560]{1,0:T(8,128)} %get-tuple-element.14.gv_ref, ...), custom_call_target="tpu_custom_call" | custom-call | flops 400000000 | bytes 4000000 | tf_op jit(solution)/shard_map/end/pallas_call | solution.py:249
  41.6 18.4 %scatter_proj.1 = f32[80,256]{1,0:T(8,128)} custom-call(bf16[8,2,80,256]{3,2,1,0:T(8,128)(2,1)} %bitcast.16), custom_call_target="tpu_custom_call" | custom-call | tf_op jit(solution)/shard_map/scatter_proj/pallas_call | solution.py:122
  60.0 1.5 %copy.10 = f32[80,256]{1,0:T(8,128)} copy(f32[80,256]{1,0:T(8,128)} %scatter_proj.1) | data formatting | bytes 163840
Async XLA Ops:
  19.5 17.2 %collective-permute-start = (bf16[128,2560]{1,0:T(8,128)(2,1)}, bf16[128,2560]{1,0:T(8,128)(2,1)S(1)}, u32[]{:S(2)}, u32[]{:S(2)}) collective-permute-start(bf16[128,2560]{1,0:T(8,128)(2,1)} %get-tuple-element.11), channel_id=1, source_target_pairs={{0,16},{16,0},{1,17},{17,1},{2,18},{18,2},{3,19},{19,3},{4,20},{20... | collective-permute-start | bytes 1966088 | tf_op jit(solution)/shard_map/ppermute | solution.py:270
  36.7 0.8 %copy-start = (bf16[128,2560]{1,0:T(8,128)(2,1)}, bf16[128,2560]{1,0:T(8,128)(2,1)S(1)}, u32[]{:S(2)}) copy-start(bf16[128,2560]{1,0:T(8,128)(2,1)S(1)} %collective-permute-done.got_ref) | copy-start | bytes 1966084

commit v2 on v1

--- a/solution.py
+++ b/solution.py
@@ -75,6 +75,9 @@
         out_specs=VM,
         scratch_shapes=sems,
         compiler_params=pltpu.CompilerParams(collective_id=0, has_side_effects=True),
+        cost_estimate=pl.CostEstimate(
+            flops=15000000000, bytes_accessed=1000000, transcendentals=0
+        ),
         name="gather_proj",
     )(shard)
     return whole.reshape(-1, shard.shape[1])
@@ -165,28 +168,30 @@
     return docs, jnp.where(docs == last, jnp.exp(columns[tokens - 1 :, :] - columns), 0.0)
 
 
-def start_kernel(len_ref, hid_ref, proj_ref, val_ref, grad_ref, dec_ref, bc_ref, pay_ref, sel_ref):
-    tokens, state = hid_ref.shape[0], proj_ref.shape[1] // 2
+def weigh_kernel(len_ref, val_ref, grad_ref, dec_ref, sel_ref):
+    tokens = val_ref.shape[0]
     lead = lax.axis_index("ctx") == 0
     first_token = lax.axis_index("ctx") * tokens
-    bc = mm(hid_ref[...], proj_ref[...]).astype(BF16)
-    bc_ref[...] = bc
     _, columns = prefix_sums(dec_ref)
     docs, out_w = out_weights(columns, len_ref, first_token)
     prev = doc_of(len_ref, jnp.full(columns.shape, first_token - 1, jnp.int32))
     in_w = jnp.where(docs == prev, jnp.exp(columns), 0.0)
-    lead_v = jnp.full((tokens, state), lead.astype(jnp.int32), jnp.int32) == 1
+    lead_v = jnp.full((tokens, 128), lead.astype(jnp.int32), jnp.int32) == 1
     weights = jnp.where(lead_v[:, : columns.shape[1]], out_w, in_w)
-    side = jnp.where(lead_v, bc[:, :state].astype(F32), bc[:, state:].astype(F32))
-    turned = (side.T).astype(BF16)
-    scale = jnp.where(lead, 1.0, 1.0 / state).astype(F32)
     low = lax.broadcasted_iota(jnp.int32, (tokens, 128), 1) < 64
     for p in range(val_ref.shape[1] // 128):
         at = slice(128 * p, 128 * p + 128)
         raw = jnp.where(lead_v, val_ref[:, at].astype(F32), grad_ref[:, at].astype(F32))
-        weighted = (raw * spread_pair(weights, 2 * p, low)).astype(BF16)
-        sel_ref[:, at] = weighted
-        pay_ref[:, at] = (mm(turned, weighted) * scale).astype(BF16)
+        sel_ref[:, at] = (raw * spread_pair(weights, 2 * p, low)).astype(BF16)
+
+
+def project_kernel(len_ref, hid_ref, proj_ref, bc_ref, side_ref):
+    tokens, state = hid_ref.shape[0], proj_ref.shape[1] // 2
+    bc = mm(hid_ref[...], proj_ref[...])
+    bc_ref[...] = bc.astype(BF16)
+    lead_v = jnp.full((tokens, state), 1 - lax.axis_index("ctx"), jnp.int32) == 1
+    side = jnp.where(lead_v, bc[:, :state], bc[:, state:])
+    side_ref[...] = side.T.astype(BF16)
 
 
 def middle_kernel(len_ref, bc_ref, val_ref, grad_ref, dec_ref, gv_ref, gbc_ref):
@@ -221,7 +226,7 @@
 
 
 def end_kernel(
-    seq_total, len_ref, got_ref, sel_ref, gv_ref, gbc_ref, bc_ref, dec_ref, proj_ref, hid_ref,
+    seq_total, len_ref, turned_ref, got_ref, sel_ref, gv_ref, gbc_ref, bc_ref, dec_ref, proj_ref, hid_ref,
     out_ref, hidden_ref, term_ref,
 ):
     tokens, state = bc_ref.shape[0], bc_ref.shape[1] // 2
@@ -230,11 +235,14 @@
     _, out_w = out_weights(columns, len_ref, lax.axis_index("ctx") * tokens)
     out_w = out_w * lead
     low = lax.broadcasted_iota(jnp.int32, (tokens, 128), 1) < 64
-    edge = mm(sel_ref[...], got_ref[...], NT)
-    b = bc_ref[:, :state]
+    edge = jnp.zeros((tokens, state), F32)
+    b, side = bc_ref[:, :state], turned_ref[...]
+    scale = lead / state + (1.0 - lead)
     for p in range(got_ref.shape[1] // 128):
         at = slice(128 * p, 128 * p + 128)
-        more = mm(b, got_ref[:, at]) * spread_pair(out_w, 2 * p, low)
+        got = (mm(side, got_ref[:, at]) * scale).astype(BF16)
+        edge = edge + mm(sel_ref[:, at], got, NT)
+        more = mm(b, got) * spread_pair(out_w, 2 * p, low)
         out_ref[:, at] = (gv_ref[:, at] + more).astype(BF16)
     gb = (gbc_ref[:, :state] + edge * lead).astype(BF16)
     gc = (gbc_ref[:, state:] + edge * ((1.0 - lead) / state)).astype(BF16)
@@ -261,13 +269,19 @@
     hid, val, dec, grad = hidden_in[0], values[0], log_decay[0], grad_out[0]
     tokens, inner = val.shape
     wide = proj_bc.shape[1]
+    swap = [(0, 1), (1, 0)]
+    (sel,) = call(
+        weigh_kernel, "weigh", 10000000, [((tokens, inner), BF16)], doc_lengths, val, grad, dec
+    )
+    sel, proj_bc = lax.optimization_barrier((sel, proj_bc))
+    got = lax.ppermute(sel, "ctx", swap)
     proj = gather(proj_bc, n)
-    bc, pay, sel = call(
-        start_kernel, "start", 200000000,
-        [((tokens, wide), BF16), ((wide // 2, inner), BF16), ((tokens, inner), BF16)],
-        doc_lengths, hid, proj, val, grad, dec,
-    )
-    got = lax.ppermute(pay, "ctx", [(0, 1), (1, 0)])
+    bc, side = call(
+        project_kernel, "project", 200000000,
+        [((tokens, wide), BF16), ((wide // 2, tokens), BF16)],
+        doc_lengths, hid, proj,
+    )
+    turned = lax.ppermute(side, "ctx", swap)
     gv, gbc = call(
         middle_kernel, "middle", 4000000000,
         [((tokens, inner), F32), ((tokens, wide), F32)],
@@ -276,7 +290,7 @@
     out, hidden, term = call(
         functools.partial(end_kernel, n * hidden_in.shape[0]), "end", 400000000,
         [((tokens, inner), BF16), (hid.shape, BF16), ((hid.shape[1], wide), BF16)],
-        doc_lengths, got, sel, gv, gbc, bc, dec, proj, hid,
+        doc_lengths, turned, got, sel, gv, gbc, bc, dec, proj, hid,
     )
     return (out[None], hidden[None], scatter_sum(term, n))
 

time: 61.8 us -> 54.7 us (0.89)
  waiting for transfers between devices: 11.7 us -> 0.01 us
  Pallas kernels: 45.3 us -> 47.8 us
  starting transfers between devices: 1.49 us -> 3.51 us
    ppermute x1 -> x2, waiting for transfers between devices: 11.7 us -> 0.01 us  [the longest x1 0.01 us: paired(): turned = lax.ppermute(side, 'ctx', swap)]
    pallas_call x3 -> x4, Pallas kernels: 12 us -> 16 us  [call(): pl.pallas_call(body, out_shape=shapes, in_specs=[SM] + [VM] * (len(args)...]
    ppermute x1 -> x2, starting transfers between devices: 1.49 us -> 3.51 us  [the longest x1 2.97 us: paired(): got = lax.ppermute(sel, 'ctx', swap)]
    pallas_call x1, Pallas kernels: 14.9 us -> 13.4 us  [gather(): pl.pallas_call(functools.partial(gather_kernel, n), out_shape=jax.ShapeDt...]
    unnamed x3 -> x5, local copies, waits for them, and re-layouts: 2.36 us -> 2.36 us
  transfers between devices with their start and end apart: 1 -> 2, of which waited for: 1 -> 0; matrix products, arithmetic and copies ran while one was open for 0% -> 0% of each run, Pallas kernels for 7% -> 36%
where the time goes in v2:
time: 54.7 us; the launch traced here: 54.3 us
  Pallas kernels  47.8 us (87%)
  starting transfers between devices  3.51 us (6%)
  local copies, waits for them, and re-layouts  2.36 us (4%)
  between operations  0.66 us (1%)
    pallas_call x1, Pallas kernels, scatter_sum(): pl.pallas_call(functools.partial(scatter_kernel, n), out_shape=jax.ShapeD...  18.3 us
    pallas_call x4, Pallas kernels, call(): pl.pallas_call(body, out_shape=shapes, in_specs=[SM] + [VM] * (len(args)...  16 us
    pallas_call x1, Pallas kernels, gather(): pl.pallas_call(functools.partial(gather_kernel, n), out_shape=jax.ShapeDt...  13.4 us
    ppermute x1, starting transfers between devices, paired(): got = lax.ppermute(sel, 'ctx', swap)  2.97 us
    unnamed x5, local copies, waits for them, and re-layouts  2.36 us
  transfers between devices with their start and end apart: 2, of which 0 were waited for; matrix products, arithmetic and copies ran while one was open for 0% of the time, Pallas kernels for 36%

profile of v2, /device:TPU:0, one launch (start us, length us, event | category | flops | bytes accessed | tf_op | source)
XLA Modules:
  0.0 54.3 jit_solution(17657594369704942147)
XLA Ops:
  0.6 3.1 %weigh.1.sel_ref = bf16[128,2560]{1,0:T(8,128)(2,1)} custom-call(s32[1,4]{1,0:T(1,128)} %len_ref.7, bf16[128,2560]{1,0:T(8,128)(2,1)} %bitcast.12, bf16[128,2560]{1,0:T(8,128)(2,1)} %bitcast.14, f32[40,128]{1,0:T(8,128)} %bitcast.17), custom_call_target="tpu_custom_call" | custom-call | flops 10000000 | bytes 4000000 | tf_op jit(solution)/shard_map/weigh/pallas_call | solution.py:257
  3.8 3.0 %collective-permute-start.1 = (bf16[128,2560]{1,0:T(8,128)(2,1)}, bf16[128,2560]{1,0:T(8,128)(2,1)S(1)}, u32[]{:S(2)}, u32[]{:S(2)}) collective-permute-start(bf16[128,2560]{1,0:T(8,128)(2,1)} %weigh.1.sel_ref), channel_id=1, source_target_pairs={{0,16},{16,0},{1,17},{17,1},{2,18},{18,2},{3,19},{19,3},{4,20},{20... | collective-permute-start | bytes 1966088 | tf_op jit(solution)/shard_map/ppermute | solution.py:277
  6.7 13.4 %gather_proj.1 = bf16[16,80,256]{2,1,0:T(8,128)(2,1)} custom-call(bf16[80,256]{1,0:T(8,128)(2,1)} %x_ref), custom_call_target="tpu_custom_call" | custom-call | flops 15000000512 | bytes 1000000 | tf_op jit(solution)/shard_map/gather_proj/pallas_call | solution.py:71
  20.2 2.2 %project.1 = (bf16[128,256]{1,0:T(8,128)(2,1)}, bf16[128,128]{1,0:T(8,128)(2,1)}) custom-call(s32[1,4]{1,0:T(1,128)} %len_ref.7, bf16[128,1280]{1,0:T(8,128)(2,1)} %bitcast.10, bf16[1280,256]{1,0:T(8,128)(2,1)} %bitcast.8), custom_call_target="tpu_custom_call" | custom-call | flops 200000000 | bytes 4000000 | tf_op jit(solution)/shard_map/project/pallas_call | solution.py:257
  22.4 0.5 collective-permute-start
  22.9 4.1 %middle.1 = (f32[128,2560]{1,0:T(8,128)}, f32[128,256]{1,0:T(8,128)}) custom-call(s32[1,4]{1,0:T(1,128)} %len_ref.7, bf16[128,256]{1,0:T(8,128)(2,1)} %get-tuple-element.15.bc_ref, bf16[128,2560]{1,0:T(8,128)(2,1)} %bitcast.13, bf16[128,2560]{1,0:T(8,128)(2,1)} %bitcast.15, f32[40,128]{1,0:T(8,128)} %bitcast.18), custom_call_target="tpu_custom_call" | custom-call | flops 4000000000 | bytes 4000000 | tf_op jit(solution)/shard_map/middle/pallas_call | solution.py:257
  26.9 0.0 collective-permute-done.turned_ref
  27.0 0.0 copy-start.1
  27.0 0.0 collective-permute-done.1.got_ref
  27.0 0.0 copy-start
  27.0 0.6 %copy-done.1 = bf16[128,128]{1,0:T(8,128)(2,1)} copy-done((bf16[128,128]{1,0:T(8,128)(2,1)}, bf16[128,128]{1,0:T(8,128)(2,1)S(1)}, u32[]{:S(2)}) %copy-start.1) | copy-done | bytes 32792
  27.6 0.2 copy-done
  27.8 6.7 %end.1 = (bf16[128,2560]{1,0:T(8,128)(2,1)}, bf16[128,1280]{1,0:T(8,128)(2,1)}, bf16[1280,256]{1,0:T(8,128)(2,1)}) custom-call(s32[1,4]{1,0:T(1,128)} %len_ref.7, bf16[128,128]{1,0:T(8,128)(2,1)} %copy-done.1, bf16[128,2560]{1,0:T(8,128)(2,1)} %copy-done, bf16[128,2560]{1,0:T(8,128)(2,1)} %weigh.1.sel_ref, f32[128,2560]{1,0:T(8,128)} %get-tuple-element.16.gv_ref, ...), custom_call_target="tpu_custom_call" | custom-call | flops 400000000 | bytes 4000000 | tf_op jit(solution)/shard_map/end/pallas_call | solution.py:257
  34.5 18.3 %scatter_proj.1 = f32[80,256]{1,0:T(8,128)} custom-call(bf16[8,2,80,256]{3,2,1,0:T(8,128)(2,1)} %bitcast.16), custom_call_target="tpu_custom_call" | custom-call | tf_op jit(solution)/shard_map/scatter_proj/pallas_call | solution.py:125
  52.8 1.5 %copy.10 = f32[80,256]{1,0:T(8,128)} copy(f32[80,256]{1,0:T(8,128)} %scatter_proj.1) | data formatting | bytes 163840
Async XLA Ops:
  3.8 23.2 %collective-permute-start.1 = (bf16[128,2560]{1,0:T(8,128)(2,1)}, bf16[128,2560]{1,0:T(8,128)(2,1)S(1)}, u32[]{:S(2)}, u32[]{:S(2)}) collective-permute-start(bf16[128,2560]{1,0:T(8,128)(2,1)} %weigh.1.sel_ref), channel_id=1, source_target_pairs={{0,16},{16,0},{1,17},{17,1},{2,18},{18,2},{3,19},{19,3},{4,20},{20... | collective-permute-start | bytes 1966088 | tf_op jit(solution)/shard_map/ppermute | solution.py:277
  22.4 4.6 %collective-permute-start = (bf16[128,128]{1,0:T(8,128)(2,1)}, bf16[128,128]{1,0:T(8,128)(2,1)S(1)}, u32[]{:S(2)}, u32[]{:S(2)}) collective-permute-start(bf16[128,128]{1,0:T(8,128)(2,1)} %get-tuple-element.13), channel_id=1, source_target_pairs={{0,16},{16,0},{1,17},{17,1},{2,18},{18,2},{3,19},{19,3},{4,20},{20... | collective-permute-start | bytes 98312 | tf_op jit(solution)/shard_map/ppermute | solution.py:284
  27.0 0.6 %copy-start.1 = (bf16[128,128]{1,0:T(8,128)(2,1)}, bf16[128,128]{1,0:T(8,128)(2,1)S(1)}, u32[]{:S(2)}) copy-start(bf16[128,128]{1,0:T(8,128)(2,1)S(1)} %collective-permute-done.turned_ref) | copy-start | bytes 98308
  27.0 0.8 %copy-start = (bf16[128,2560]{1,0:T(8,128)(2,1)}, bf16[128,2560]{1,0:T(8,128)(2,1)S(1)}, u32[]{:S(2)}) copy-start(bf16[128,2560]{1,0:T(8,128)(2,1)S(1)} %collective-permute-done.1.got_ref) | copy-start | bytes 1966084
